TPU v7x, 32 devices: a whole 2x2x4 slice. The times are simulated.
32 devices in a mesh: fsdp: 8 (over z, x), dp: 4 (over y, core).
Axes of the slice: x: 2, y: 2, z: 4, core: 2. Of those that a mesh axis runs over, the one named last changes fastest.
Arguments:
- hidden: bfloat16 [2, 32, 384, 1536], P(None, ('fsdp', 'dp')), may hold values from -6 to 6
- teacher: bfloat16 [2, 32, 384, 1536], P(None, ('fsdp', 'dp')), may hold values from -6 to 6
- cotangent: bfloat16 [2, 32, 384, 1536], P(None, ('fsdp', 'dp')), may hold values from -6.3329935e-07 to 6.3329935e-07
- valid_mask: int32 [2, 32, 384], P(None, ('fsdp', 'dp')), may hold values from 0 to 1, as said below
- blocks: int32 [2, 32, 384], P(None, ('fsdp', 'dp')), may hold values from 0 to 2, never falling along the last dimension, each value on 1 to 256 neighbouring positions
- buckets: int32 [384, 384], replicated, may hold values from 0 to 31
- first_gain: bfloat16 [1536], P(('fsdp', 'dp')), may hold values from 0.25 to 1.75
- query_weight: bfloat16 [1536, 768], P('fsdp', 'dp'), may hold values from -0.0390625 to 0.0390625
- key_weight: bfloat16 [1536, 768], P('fsdp', 'dp'), may hold values from -0.15625 to 0.15625
- value_weight: bfloat16 [1536, 768], P('fsdp', 'dp'), may hold values from -0.15625 to 0.15625
- output_weight: bfloat16 [1536, 768], P('fsdp', 'dp'), may hold values from -1.25 to 1.25
- second_gain: bfloat16 [1536], P(('fsdp', 'dp')), may hold values from 0.25 to 1.75
- gate_weight: bfloat16 [1536, 3968], P('fsdp', 'dp'), may hold values from -0.15625 to 0.15625
- up_weight: bfloat16 [1536, 3968], P('fsdp', 'dp'), may hold values from -0.15625 to 0.15625
- down_weight: bfloat16 [1536, 3968], P('fsdp', 'dp'), may hold values from -0.1875 to 0.1875
- bias_table: bfloat16 [32, 12], replicated, may hold values from -5 to 5
Outputs:
- layer_output: bfloat16 [2, 32, 384, 1536], P(None, ('fsdp', 'dp'))
- loss_value: float32 [], replicated
- hidden_grad: bfloat16 [2, 32, 384, 1536], P(None, ('fsdp', 'dp'))
- first_gain_grad: float32 [1536], P(('fsdp', 'dp'))
- query_grad: float32 [1536, 768], P('fsdp', 'dp')
- key_grad: float32 [1536, 768], P('fsdp', 'dp')
- value_grad: float32 [1536, 768], P('fsdp', 'dp')
- output_grad: float32 [1536, 768], P('fsdp', 'dp')
- second_gain_grad: float32 [1536], P(('fsdp', 'dp'))
- gate_grad: float32 [1536, 3968], P('fsdp', 'dp')
- up_grad: float32 [1536, 3968], P('fsdp', 'dp')
- down_grad: float32 [1536, 3968], P('fsdp', 'dp')
- bias_grad: float32 [32, 12], replicated
Inputs may be any that keep to these rules, and one draw needn't show every extreme that they name: `valid_mask`: 1 marks a valid token. `blocks`: never falls along a sequence; every block number up to the largest occurs, each block has 1 to 256 positions and some block has exactly 256.
All inputs are finite; a program needn't handle non-finite values.
Results may differ from a plain program's by a relative error of at most 0.013.
The roundings to bfloat16 on the way count: a program that leaves them out, or rounds other values in their place, can miss the bound.
Values may be sent and summed in bfloat16 or wider, within the bound.
A program may use at most 320 MiB of HBM per device.

v0:
```python
import jax
import jax.numpy as jnp
from jax import lax
from jax.sharding import PartitionSpec as P

EPS = 1e-06
NEG = -1000000000.0
HIGH = lax.Precision.HIGHEST


def times_rows(former, latter):
    return jnp.dot(former, latter, preferred_element_type=jnp.float32)


def times_transpose(former, latter):
    return lax.dot_general(
        former, latter, (((1,), (1,)), ((), ())), preferred_element_type=jnp.float32
    )


def over_tokens(former, latter):
    return lax.dot_general(
        former, latter, (((0,), (0,)), ((), ())), preferred_element_type=jnp.float32
    )


def assemble(gathered, fsdp_count, dp_count):
    row_block = gathered.shape[0] // (fsdp_count * dp_count)
    col_block = gathered.shape[1]
    shaped = gathered.reshape(fsdp_count, dp_count, row_block, col_block)
    return jnp.transpose(shaped, (0, 2, 1, 3)).reshape(fsdp_count * row_block, dp_count * col_block)


def disperse(gradient, fsdp_count, dp_count):
    row_block = gradient.shape[0] // fsdp_count
    col_block = gradient.shape[1] // dp_count
    shaped = gradient.reshape(fsdp_count, row_block, dp_count, col_block)
    return jnp.transpose(shaped, (0, 2, 1, 3)).reshape(fsdp_count * dp_count * row_block, col_block)


def norm_forward(inputs, norm_gain):
    row_scale = lax.rsqrt(jnp.mean(inputs * inputs, axis=-1, keepdims=True) + EPS)
    return (inputs * row_scale * norm_gain, row_scale)


def norm_backward(inputs, row_scale, norm_gain, upstream):
    scaled = upstream * norm_gain
    gain_grad = jnp.sum(upstream * inputs * row_scale, axis=0)
    mean_term = jnp.mean(scaled * inputs, axis=-1, keepdims=True)
    return (
        row_scale * scaled - inputs * (row_scale * row_scale * row_scale) * mean_term,
        gain_grad,
    )


def gelu_tanh(values_in):
    return jax.nn.gelu(values_in, approximate=True)


def masked_scores(queries, key_heads, position_bias, allowed):
    products = jnp.einsum("qhd,khd->hqk", queries, key_heads, preferred_element_type=jnp.float32)
    return jnp.where(allowed[None], products + position_bias, NEG)


def body(
    hidden,
    teacher,
    cotangent,
    valid_mask,
    blocks,
    buckets,
    first_gain,
    query_weight,
    key_weight,
    value_weight,
    output_weight,
    second_gain,
    gate_weight,
    up_weight,
    down_weight,
    bias_table,
):
    fsdp_count = lax.axis_size("fsdp")
    dp_count = lax.axis_size("dp")
    micro_count = hidden.shape[0]
    seq_len = hidden.shape[2]
    model_width = hidden.shape[3]
    bucket_count = bias_table.shape[0]
    head_count = bias_table.shape[1]
    scale_factor = jnp.float32(
        float(micro_count * lax.axis_size(("fsdp", "dp")) * hidden.shape[1] * seq_len * model_width)
    )
    valid_float = valid_mask.astype(jnp.float32)
    valid_total = lax.psum(jnp.sum(valid_float), ("fsdp", "dp"))
    places = lax.broadcasted_iota(jnp.int32, (1, 1, bucket_count), 2)
    onehot = (buckets[:, :, None] == places).astype(jnp.float32)
    position_bias = jnp.einsum(
        "qkb,bh->hqk", onehot, bias_table.astype(jnp.float32), precision=HIGH
    )
    onehot_low = onehot.astype(jnp.bfloat16)
    rows_iota = lax.broadcasted_iota(jnp.int32, (seq_len, seq_len), 0)
    cols_iota = lax.broadcasted_iota(jnp.int32, (seq_len, seq_len), 1)
    diagonal = rows_iota == cols_iota

    def rebuild(gathered):
        return (gathered[0],) + tuple(
            (assemble(matrix, fsdp_count, dp_count) for matrix in gathered[1:])
        )

    def spread_out(grads):
        return (
            (grads[0],)
            + tuple((disperse(matrix, fsdp_count, dp_count) for matrix in grads[1:5]))
            + (grads[5],)
            + tuple((disperse(matrix, fsdp_count, dp_count) for matrix in grads[6:]))
        )

    outputs_list = []
    input_grads = []
    squares = jnp.float32(0.0)
    table_grad = jnp.zeros((bucket_count, head_count), jnp.float32)
    totals = None
    for step_index in range(micro_count):
        inputs = hidden[step_index, 0].astype(jnp.float32)
        target = teacher[step_index, 0].astype(jnp.float32)
        upstream = cotangent[step_index, 0].astype(jnp.float32)
        token_valid = valid_float[step_index, 0]
        block_ids = blocks[step_index, 0]
        allowed = (block_ids[None, :] <= block_ids[:, None]) & (
            valid_mask[step_index, 0][None, :] == 1
        ) | diagonal
        first_block = rebuild(
            (
                lax.all_gather(first_gain, ("fsdp", "dp"), axis=0, tiled=True),
                lax.all_gather(query_weight, ("fsdp", "dp"), axis=0, tiled=True),
                lax.all_gather(key_weight, ("fsdp", "dp"), axis=0, tiled=True),
                lax.all_gather(value_weight, ("fsdp", "dp"), axis=0, tiled=True),
                lax.all_gather(output_weight, ("fsdp", "dp"), axis=0, tiled=True),
            )
        )
        gain_one = first_block[0].astype(jnp.float32)
        normed_full, scale_one = norm_forward(inputs, gain_one)
        normed_one = normed_full.astype(jnp.bfloat16)
        head_size = first_block[1].shape[1] // head_count
        head_split = (seq_len, head_count, head_size)
        queries = times_rows(normed_one, first_block[1]).astype(jnp.bfloat16).reshape(head_split)
        key_heads = times_rows(normed_one, first_block[2]).astype(jnp.bfloat16).reshape(head_split)
        value_heads = (
            times_rows(normed_one, first_block[3]).astype(jnp.bfloat16).reshape(head_split)
        )
        scores = masked_scores(queries, key_heads, position_bias, allowed)
        row_max = jnp.max(scores, axis=-1, keepdims=True)
        exponent = jnp.exp(scores - row_max)
        row_total = jnp.sum(exponent, axis=-1, keepdims=True)
        log_total = row_max + jnp.log(row_total)
        softmax_low = (exponent / row_total).astype(jnp.bfloat16)
        attended = jnp.einsum(
            "hqk,khd->qhd", softmax_low, value_heads, preferred_element_type=jnp.float32
        )
        attended = attended.astype(jnp.bfloat16).reshape(seq_len, head_count * head_size)
        middle = inputs + times_transpose(attended, first_block[4])
        second_block = rebuild(
            (
                lax.all_gather(second_gain, ("fsdp", "dp"), axis=0, tiled=True),
                lax.all_gather(gate_weight, ("fsdp", "dp"), axis=0, tiled=True),
                lax.all_gather(up_weight, ("fsdp", "dp"), axis=0, tiled=True),
                lax.all_gather(down_weight, ("fsdp", "dp"), axis=0, tiled=True),
            )
        )
        gain_two = second_block[0].astype(jnp.float32)
        normed_mid, scale_two = norm_forward(middle, gain_two)
        normed_two = normed_mid.astype(jnp.bfloat16)
        gate_pre = times_rows(normed_two, second_block[1])
        up_pre = times_rows(normed_two, second_block[2])
        gate_act, gelu_pullback = jax.vjp(gelu_tanh, gate_pre)
        hidden_act = (gate_act * up_pre).astype(jnp.bfloat16)
        layer_full = middle + times_transpose(hidden_act, second_block[3])
        outputs_list.append(layer_full.astype(jnp.bfloat16))
        residual_gap = layer_full - target
        weighted_gap = token_valid[:, None] * residual_gap
        squares = squares + jnp.sum(weighted_gap * residual_gap)
        grad_out = scale_factor * upstream + scale_factor * (
            2.0 * weighted_gap / (valid_total * model_width)
        )
        back_second = rebuild(
            (
                lax.all_gather(second_gain, ("fsdp", "dp"), axis=0, tiled=True),
                lax.all_gather(gate_weight, ("fsdp", "dp"), axis=0, tiled=True),
                lax.all_gather(up_weight, ("fsdp", "dp"), axis=0, tiled=True),
                lax.all_gather(down_weight, ("fsdp", "dp"), axis=0, tiled=True),
            )
        )
        grad_ffn = grad_out.astype(jnp.bfloat16)
        down_part = over_tokens(grad_ffn, hidden_act)
        grad_hidden_act = times_rows(grad_ffn, back_second[3])
        grad_gate = gelu_pullback(grad_hidden_act * up_pre)[0].astype(jnp.bfloat16)
        grad_up = (grad_hidden_act * gate_act).astype(jnp.bfloat16)
        gate_part = over_tokens(normed_two, grad_gate)
        up_part = over_tokens(normed_two, grad_up)
        grad_normed_two = times_transpose(grad_gate, back_second[1]) + times_transpose(
            grad_up, back_second[2]
        )
        middle_term, gain_two_part = norm_backward(
            middle, scale_two, back_second[0].astype(jnp.float32), grad_normed_two
        )
        grad_middle = grad_out + middle_term
        grad_attn = grad_middle.astype(jnp.bfloat16)
        back_first = rebuild(
            (
                lax.all_gather(first_gain, ("fsdp", "dp"), axis=0, tiled=True),
                lax.all_gather(query_weight, ("fsdp", "dp"), axis=0, tiled=True),
                lax.all_gather(key_weight, ("fsdp", "dp"), axis=0, tiled=True),
                lax.all_gather(value_weight, ("fsdp", "dp"), axis=0, tiled=True),
                lax.all_gather(output_weight, ("fsdp", "dp"), axis=0, tiled=True),
            )
        )
        output_part = over_tokens(grad_attn, attended)
        grad_attended = (
            times_rows(grad_attn, back_first[4]).astype(jnp.bfloat16).reshape(head_split)
        )
        scores_again = masked_scores(queries, key_heads, position_bias, allowed)
        softmax_again = jnp.exp(scores_again - log_total)
        grad_probs = jnp.einsum(
            "qhd,khd->hqk", grad_attended, value_heads, preferred_element_type=jnp.float32
        )
        grad_scores = softmax_again * (
            grad_probs - jnp.sum(softmax_again * grad_probs, axis=-1, keepdims=True)
        )
        grad_scores = grad_scores.astype(jnp.bfloat16)
        table_grad = table_grad + jnp.einsum(
            "hqk,qkb->bh", grad_scores, onehot_low, preferred_element_type=jnp.float32
        )
        flat_width = head_count * head_size
        grad_queries = (
            jnp.einsum("hqk,khd->qhd", grad_scores, key_heads, preferred_element_type=jnp.float32)
            .astype(jnp.bfloat16)
            .reshape(seq_len, flat_width)
        )
        grad_keys = (
            jnp.einsum("hqk,qhd->khd", grad_scores, queries, preferred_element_type=jnp.float32)
            .astype(jnp.bfloat16)
            .reshape(seq_len, flat_width)
        )
        grad_values = (
            jnp.einsum(
                "hqk,qhd->khd",
                softmax_again.astype(jnp.bfloat16),
                grad_attended,
                preferred_element_type=jnp.float32,
            )
            .astype(jnp.bfloat16)
            .reshape(seq_len, flat_width)
        )
        query_part = over_tokens(normed_one, grad_queries)
        key_part = over_tokens(normed_one, grad_keys)
        value_part = over_tokens(normed_one, grad_values)
        grad_normed_one = (
            times_transpose(grad_queries, back_first[1])
            + times_transpose(grad_keys, back_first[2])
            + times_transpose(grad_values, back_first[3])
        )
        input_term, gain_one_part = norm_backward(
            inputs, scale_one, back_first[0].astype(jnp.float32), grad_normed_one
        )
        input_grads.append((grad_middle + input_term).astype(jnp.bfloat16))
        step_set = spread_out(
            (
                gain_one_part,
                query_part,
                key_part,
                value_part,
                output_part,
                gain_two_part,
                gate_part,
                up_part,
                down_part,
            )
        )
        totals = step_set if totals is None else jax.tree.map(jnp.add, totals, step_set)
    shards = (
        lax.psum_scatter(totals[0], ("fsdp", "dp"), scatter_dimension=0, tiled=True),
        lax.psum_scatter(totals[1], ("fsdp", "dp"), scatter_dimension=0, tiled=True),
        lax.psum_scatter(totals[2], ("fsdp", "dp"), scatter_dimension=0, tiled=True),
        lax.psum_scatter(totals[3], ("fsdp", "dp"), scatter_dimension=0, tiled=True),
        lax.psum_scatter(totals[4], ("fsdp", "dp"), scatter_dimension=0, tiled=True),
        lax.psum_scatter(totals[5], ("fsdp", "dp"), scatter_dimension=0, tiled=True),
        lax.psum_scatter(totals[6], ("fsdp", "dp"), scatter_dimension=0, tiled=True),
        lax.psum_scatter(totals[7], ("fsdp", "dp"), scatter_dimension=0, tiled=True),
        lax.psum_scatter(totals[8], ("fsdp", "dp"), scatter_dimension=0, tiled=True),
    )
    total_squares, table_all = lax.psum((squares, table_grad), ("fsdp", "dp"))
    loss_value = total_squares / (valid_total * model_width)
    layer_output = jnp.stack(outputs_list)[:, None]
    hidden_grad = jnp.stack(input_grads)[:, None]
    return (
        layer_output,
        loss_value,
        hidden_grad,
        shards[0],
        shards[1],
        shards[2],
        shards[3],
        shards[4],
        shards[5],
        shards[6],
        shards[7],
        shards[8],
        table_all,
    )


def solution(mesh):
    in_specs = (
        P(None, ("fsdp", "dp"), None, None),
        P(None, ("fsdp", "dp"), None, None),
        P(None, ("fsdp", "dp"), None, None),
        P(None, ("fsdp", "dp"), None),
        P(None, ("fsdp", "dp"), None),
        P(),
        P(("fsdp", "dp")),
        P("fsdp", "dp"),
        P("fsdp", "dp"),
        P("fsdp", "dp"),
        P("fsdp", "dp"),
        P(("fsdp", "dp")),
        P("fsdp", "dp"),
        P("fsdp", "dp"),
        P("fsdp", "dp"),
        P(),
    )
    out_specs = (
        P(None, ("fsdp", "dp"), None, None),
        P(),
        P(None, ("fsdp", "dp"), None, None),
        P(("fsdp", "dp")),
        P("fsdp", "dp"),
        P("fsdp", "dp"),
        P("fsdp", "dp"),
        P("fsdp", "dp"),
        P(("fsdp", "dp")),
        P("fsdp", "dp"),
        P("fsdp", "dp"),
        P("fsdp", "dp"),
        P(),
    )
    return jax.shard_map(body, mesh=mesh, in_specs=in_specs, out_specs=out_specs, check_vma=False)
```

profile of v0, /device:TPU:0, one launch (start us, length us, event | category | flops | bytes accessed | tf_op | source)
XLA Modules:
  0.0 2003.4 jit_solution(12041364364537936734)
XLA Ops:
  13.3 42.2 %psum.22 = f32[]{:T(128)} all-reduce(f32[]{:T(128)} %convert_reduce_fusion), channel_id=1, replica_groups=mesh['fsdp'=8,'dp'=4] {'fsdp','dp'}, use_global_device_ids=true, to_apply=%region_12.13 | all-reduce | flops 1 | bytes 8 | tf_op jit(solution)/shard_map/psum | solution.py:94
  57.9 40.4 %all-reduce.5 = (bf16[1536]{0:T(1024)(128)(2,1)S(1)}, bf16[1536]{0:T(1024)(128)(2,1)S(1)}) all-reduce(bf16[1536]{0:T(1024)(128)(2,1)S(1)} %dynamic-update-slice, bf16[1536]{0:T(1024)(128)(2,1)S(1)} %dynamic-update-slice.1), channel_id=1, replica_groups=mesh['fsdp'=8,'dp'=4] {'fsdp','dp'}, use_global_device_ids=true, to_apply=%add | all-reduce | flops 3072 | bytes 12288
  114.5 6.1 reshape.535
  120.6 13.0 all-gather.12.cloned.1.call-done
  145.1 49.3 %all-gather.8.cloned.1.call-done = bf16[6144,192]{1,0:T(8,128)(2,1)} async-done(((bf16[192,192]{1,0:T(8,128)(2,1)}), bf16[6144,192]{1,0:T(8,128)(2,1)}) %all-gather.8.cloned.1.call-update) | async-done | bytes 2359312 | tf_op jit(solution)/shard_map/all_gather | solution.py:137
  205.9 49.1 %all-gather.14.cloned.1.call-done = bf16[6144,192]{1,0:T(8,128)(2,1)} async-done(((bf16[192,192]{1,0:T(8,128)(2,1)}), bf16[6144,192]{1,0:T(8,128)(2,1)}) %all-gather.14.cloned.1.call-update) | async-done | bytes 2359312 | tf_op jit(solution)/shard_map/all_gather | solution.py:138
  260.6 6.5 reshape.542
  298.9 7.2 fusion.119
  327.8 24.9 %all-gather.16.cloned.1.call-done = bf16[6144,992]{1,0:T(8,128)(2,1)} async-done(((bf16[192,992]{1,0:T(8,128)(2,1)}), bf16[6144,992]{1,0:T(8,128)(2,1)}) %all-gather.16.cloned.1.call-update) | async-done | bytes 12189712 | tf_op jit(solution)/shard_map/all_gather | solution.py:165
  352.6 15.6 copy.177
  368.2 25.0 %reshape.544 = bf16[1536,3968]{1,0:T(8,128)(2,1)} reshape(bf16[8,192,4,992]{3,2,1,0:T(4,128)(2,1)} %bitcast.396) | data formatting | bytes 24379392 | tf_op jit(solution)/shard_map/reshape | solution.py:31
  393.2 56.5 %all-gather.18.cloned.1.call-done = bf16[6144,992]{1,0:T(8,128)(2,1)} async-done(((bf16[192,992]{1,0:T(8,128)(2,1)}), bf16[6144,992]{1,0:T(8,128)(2,1)}) %all-gather.18.cloned.1.call-update) | async-done | bytes 12189712 | tf_op jit(solution)/shard_map/all_gather | solution.py:166
  449.7 15.6 copy.176
  465.3 25.2 %reshape.546 = bf16[1536,3968]{1,0:T(8,128)(2,1)} reshape(bf16[8,192,4,992]{3,2,1,0:T(4,128)(2,1)} %bitcast.397) | data formatting | bytes 24379392 | tf_op jit(solution)/shard_map/reshape | solution.py:31
  490.5 56.4 %all-gather.20.cloned.1.call-done = bf16[6144,992]{1,0:T(8,128)(2,1)} async-done(((bf16[192,992]{1,0:T(8,128)(2,1)}), bf16[6144,992]{1,0:T(8,128)(2,1)}) %all-gather.20.cloned.1.call-update) | async-done | bytes 12189712 | tf_op jit(solution)/shard_map/all_gather | solution.py:167
  546.8 15.6 copy.175
  562.5 25.0 %reshape.548 = bf16[1536,3968]{1,0:T(8,128)(2,1)} reshape(bf16[8,192,4,992]{3,2,1,0:T(4,128)(2,1)} %bitcast.398) | data formatting | bytes 24379392 | tf_op jit(solution)/shard_map/reshape | solution.py:31
  587.4 11.9 fusion.121
  599.3 11.8 fusion.122
  611.1 9.2 multiply_convert_fusion.4
  620.3 11.4 multiply_convert_fusion.5
  631.8 9.9 convolution_add_fusion.11
  641.7 13.7 fusion.74
  655.4 17.2 multiply_convert_fusion.3
  672.6 10.8 fusion.123
  683.4 15.5 multiply_convert_fusion.2
  698.9 10.8 fusion.125
  709.8 9.9 convolution_add_fusion.10
  719.7 19.5 multiply_reduce_fusion.2
  765.7 7.3 multiply_reduce_fusion.1
  773.0 7.1 multiply_convert_fusion.1
  837.8 14.0 fusion.106
  851.8 17.0 convolution_add_fusion
  868.8 32.5 %add.290 = f32[8,192,4,992]{3,2,1,0:T(4,128)} reshape(f32[1536,3968]{1,0:T(8,128)} %convolution_add_fusion) | data formatting | bytes 48758784 | tf_op jit(solution)/shard_map/add | solution.py:279
  901.4 25.3 %copy.140 = f32[8,4,192,992]{3,2,1,0:T(8,128)} copy(f32[8,4,192,992]{3,1,2,0:T(4,128)} %bitcast.393) | data formatting | bytes 48758784 | tf_op jit(solution)/shard_map/add | solution.py:279
  928.0 13.5 fusion.132
  941.5 17.0 convolution_add_fusion.1
  958.5 32.6 %add.286 = f32[8,192,4,992]{3,2,1,0:T(4,128)} reshape(f32[1536,3968]{1,0:T(8,128)} %convolution_add_fusion.1) | data formatting | bytes 48758784 | tf_op jit(solution)/shard_map/add | solution.py:279
  991.1 24.9 %copy.139 = f32[8,4,192,992]{3,2,1,0:T(8,128)} copy(f32[8,4,192,992]{3,1,2,0:T(4,128)} %bitcast.394) | data formatting | bytes 48758784 | tf_op jit(solution)/shard_map/add | solution.py:279
  1016.2 14.0 fusion.131
  1030.2 17.5 convolution_add_fusion.2
  1047.8 32.6 %add.282 = f32[8,192,4,992]{3,2,1,0:T(4,128)} reshape(f32[1536,3968]{1,0:T(8,128)} %convolution_add_fusion.2) | data formatting | bytes 48758784 | tf_op jit(solution)/shard_map/add | solution.py:279
  1080.3 25.2 %copy.138 = f32[8,4,192,992]{3,2,1,0:T(8,128)} copy(f32[8,4,192,992]{3,1,2,0:T(4,128)} %bitcast.395) | data formatting | bytes 48758784 | tf_op jit(solution)/shard_map/add | solution.py:279
  1116.8 40.0 %all-reduce.4 = (f32[]{:T(128)}, f32[1536]{0:T(1024)}, f32[1536]{0:T(1024)}, f32[32,12]{0,1:T(8,128)}) all-reduce(f32[]{:T(128)S(6)} %add.252, f32[1536]{0:T(1024)} %add.267, f32[1536]{0:T(1024)} %add.280, f32[32,12]{0,1:T(8,128)} %fusion.98), channel_id=1, replica_groups=mesh['fsdp'=8,'dp'=4] {'fsdp','dp'}, use_global_device_ids=true, to_apply=%region_10.11 | all-reduce | flops 3457 | bytes 27656 | tf_op jit(solution)/shard_map/psum | solution.py:291
  1169.0 69.7 %reduce-scatter.8.cloned.1.call-done = f32[192,192]{1,0:T(8,128)} async-done(((f32[6144,192]{1,0:T(8,128)}), f32[192,192]{1,0:T(8,128)}) %reduce-scatter.8.cloned.1.call-update) | async-done | bytes 147472 | tf_op jit(solution)/shard_map/reduce_scatter | solution.py:282
  1238.7 251.5 %reduce-scatter.20.cloned.1.call-done = f32[192,992]{1,0:T(8,128)} async-done(((f32[6144,992]{1,0:T(8,128)}), f32[192,992]{1,0:T(8,128)}) %reduce-scatter.20.cloned.1.call-update) | async-done | bytes 761872 | tf_op jit(solution)/shard_map/reduce_scatter | solution.py:289
  1490.2 253.2 %reduce-scatter.18.cloned.1.call-done = f32[192,992]{1,0:T(8,128)} async-done(((f32[6144,992]{1,0:T(8,128)}), f32[192,992]{1,0:T(8,128)}) %reduce-scatter.18.cloned.1.call-update) | async-done | bytes 761872 | tf_op jit(solution)/shard_map/reduce_scatter | solution.py:288
  1743.4 251.9 %reduce-scatter.16.cloned.1.call-done = f32[192,992]{1,0:T(8,128)} async-done(((f32[6144,992]{1,0:T(8,128)}), f32[192,992]{1,0:T(8,128)}) %reduce-scatter.16.cloned.1.call-update) | async-done | bytes 761872 | tf_op jit(solution)/shard_map/reduce_scatter | solution.py:287
  (333 shorter events, 212.0 us)
Async XLA Ops:
  7.2 96.6 %copy-start = (bf16[32,12]{0,1:T(8,128)(2,1)S(1)}, bf16[32,12]{0,1:T(8,128)(2,1)}, u32[]{:S(2)}) copy-start(bf16[32,12]{0,1:T(8,128)(2,1)} %param.31) | copy-start | bytes 2308
  7.2 94.3 %copy-start.75 = (s32[2,1,384]{2,1,0:T(1,128)S(1)}, s32[2,1,384]{2,1,0:T(1,128)}, u32[]{:S(2)}) copy-start(s32[2,1,384]{2,1,0:T(1,128)} %param.19) | copy-start | bytes 9220
  7.2 94.3 %copy-start.89 = (s32[2,1,384]{2,1,0:T(1,128)S(1)}, s32[2,1,384]{2,1,0:T(1,128)}, u32[]{:S(2)}) copy-start(s32[2,1,384]{2,1,0:T(1,128)} %param.20) | copy-start | bytes 9220
  7.2 94.3 %copy-start.4 = (bf16[2,1,384,1536]{3,2,1,0:T(8,128)(2,1)S(1)}, bf16[2,1,384,1536]{3,2,1,0:T(8,128)(2,1)}, u32[]{:S(2)}) copy-start(bf16[2,1,384,1536]{3,2,1,0:T(8,128)(2,1)} %param.16) | copy-start | bytes 7077892
  7.2 101.8 %all-gather.10.cloned.1.call-start = ((), (), s32[]{:S(2)}) async-start(), calls=%async_computation.8 | async-start | bytes 3244032 | tf_op jit(solution)/shard_map/all_gather | solution.py:135
  8.0 125.6 %all-gather.12.cloned.1.call-start = ((), (), s32[]{:S(2)}) async-start(), calls=%async_computation.9 | async-start | bytes 3244032 | tf_op jit(solution)/shard_map/all_gather | solution.py:136
  8.7 185.7 %all-gather.8.cloned.1.call-start = ((), (), s32[]{:S(2)}) async-start(), calls=%async_computation.7 | async-start | bytes 3244032 | tf_op jit(solution)/shard_map/all_gather | solution.py:137
  9.4 245.6 %all-gather.14.cloned.1.call-start = ((), (), s32[]{:S(2)}) async-start(), calls=%async_computation.10 | async-start | bytes 3244032 | tf_op jit(solution)/shard_map/all_gather | solution.py:138
  10.0 342.6 %all-gather.16.cloned.1.call-start = ((), (), s32[]{:S(2)}) async-start(), calls=%async_computation.11 | async-start | bytes 12976128 | tf_op jit(solution)/shard_map/all_gather | solution.py:165
  10.6 439.1 %all-gather.18.cloned.1.call-start = ((), (), s32[]{:S(2)}) async-start(), calls=%async_computation.12 | async-start | bytes 12976128 | tf_op jit(solution)/shard_map/all_gather | solution.py:166
  11.2 535.7 %all-gather.20.cloned.1.call-start = ((), (), s32[]{:S(2)}) async-start(), calls=%async_computation.13 | async-start | bytes 12976128 | tf_op jit(solution)/shard_map/all_gather | solution.py:167
  11.9 1157.1 %reduce-scatter.14.cloned.1.call-start = ((), (), s32[]{:S(2)}) async-start(), calls=%async_computation.17 | async-start | bytes 6488064 | tf_op jit(solution)/shard_map/reduce_scatter | solution.py:285
  98.9 228.4 %copy-start.69 = (f32[1536]{0:T(1024)}, f32[1536]{0:T(1024)S(1)}, u32[]{:S(2)}) copy-start(f32[1536]{0:T(1024)S(1)} %convert_element_type.234) | copy-start | bytes 18436
  102.7 172.8 %copy-start.76 = (f32[384]{0:T(512)}, f32[384]{0:T(512)S(1)}, u32[]{:S(2)}) copy-start(f32[384]{0:T(512)S(1)} %get-tuple-element.103) | copy-start | bytes 4612
  270.2 28.6 %copy-start.34 = (bf16[384,768]{0,1:T(8,128)(2,1)}, bf16[384,768]{0,1:T(8,128)(2,1)S(1)}, u32[]{:S(2)}) copy-start(bf16[384,768]{0,1:T(8,128)(2,1)S(1)} %copy.124) | copy-start | bytes 1769476
  275.5 23.4 %copy-start.36 = (bf16[384,768]{0,1:T(8,128)(2,1)}, bf16[384,768]{0,1:T(8,128)(2,1)S(1)}, u32[]{:S(2)}) copy-start(bf16[384,768]{0,1:T(8,128)(2,1)S(1)} %copy.123) | copy-start | bytes 1769476
  314.0 13.3 copy-start.11
  314.6 12.7 copy-start.82
  327.7 283.3 %copy-start.24 = (bf16[384,1536]{1,0:T(8,128)(2,1)}, bf16[384,1536]{1,0:T(8,128)(2,1)S(1)}, u32[]{:S(2)}) copy-start(bf16[384,1536]{1,0:T(8,128)(2,1)S(1)} %get-tuple-element.99) | copy-start | bytes 3538948
  327.7 292.6 %copy-start.28 = (bf16[384,1536]{1,0:T(8,128)(2,1)}, bf16[384,1536]{1,0:T(8,128)(2,1)S(1)}, u32[]{:S(2)}) copy-start(bf16[384,1536]{1,0:T(8,128)(2,1)S(1)} %get-tuple-element.98) | copy-start | bytes 3538948
  587.4 23.6 %slice-start.7 = ((s8[12189696]{0:T(1024)(128)(4,1)}), s8[4194304]{0:T(1024)(128)(4,1)S(1)}, s32[]{:S(2)}) async-start(s8[12189696]{0:T(1024)(128)(4,1)} %bitcast.416), calls=%async_computation.28 | async-start | bytes 8388608
  587.4 23.7 %slice-start.8 = ((s8[12189696]{0:T(1024)(128)(4,1)}), s8[4194304]{0:T(1024)(128)(4,1)S(1)}, s32[]{:S(2)}) async-start(s8[12189696]{0:T(1024)(128)(4,1)} %bitcast.416), calls=%async_computation.29 | async-start | bytes 8388608
  599.3 11.8 slice-start.9
  620.3 11.4 copy-start.56
  620.3 11.4 copy-start.12
  655.4 83.8 %copy-start.26 = (f32[384,1536]{1,0:T(8,128)}, f32[384,1536]{1,0:T(8,128)S(1)}, u32[]{:S(2)}) copy-start(f32[384,1536]{1,0:T(8,128)S(1)} %get-tuple-element.86) | copy-start | bytes 7077892
  655.4 83.8 %copy-start.30 = (f32[384,1536]{1,0:T(8,128)}, f32[384,1536]{1,0:T(8,128)S(1)}, u32[]{:S(2)}) copy-start(f32[384,1536]{1,0:T(8,128)S(1)} %get-tuple-element.87) | copy-start | bytes 7077892
  698.9 10.8 copy-start.55
  698.9 10.8 copy-start.54
  698.9 10.8 copy-start.92
  719.7 19.5 copy-start.86
  719.7 19.5 copy-start.87
  753.7 11.4 copy-start.44
  755.3 27.1 %copy-start.42 = (bf16[384,768]{0,1:T(8,128)(2,1)}, bf16[384,768]{0,1:T(8,128)(2,1)S(1)}, u32[]{:S(2)}) copy-start(bf16[384,768]{0,1:T(8,128)(2,1)S(1)} %copy.130) | copy-start | bytes 1769476
  764.7 404.4 %reduce-scatter.12.cloned.1.call-start = ((), (), s32[]{:S(2)}) async-start(), calls=%async_computation.16 | async-start | bytes 6488064 | tf_op jit(solution)/shard_map/reduce_scatter | solution.py:284
  822.4 346.6 %reduce-scatter.10.cloned.1.call-start = ((), (), s32[]{:S(2)}) async-start(), calls=%async_computation.15 | async-start | bytes 6488064 | tf_op jit(solution)/shard_map/reduce_scatter | solution.py:283
  829.9 408.8 %reduce-scatter.8.cloned.1.call-start = ((), (), s32[]{:S(2)}) async-start(), calls=%async_computation.14 | async-start | bytes 6488064 | tf_op jit(solution)/shard_map/reduce_scatter | solution.py:282
  837.3 14.5 copy-start.27
  837.3 652.9 %reduce-scatter.20.cloned.1.call-start = ((), (), s32[]{:S(2)}) async-start(), calls=%async_computation.20 | async-start | bytes 25952256 | tf_op jit(solution)/shard_map/reduce_scatter | solution.py:289
  926.7 14.8 copy-start.25
  926.7 816.7 %reduce-scatter.18.cloned.1.call-start = ((), (), s32[]{:S(2)}) async-start(), calls=%async_computation.19 | async-start | bytes 25952256 | tf_op jit(solution)/shard_map/reduce_scatter | solution.py:288
  1016.0 979.3 %reduce-scatter.16.cloned.1.call-start = ((), (), s32[]{:S(2)}) async-start(), calls=%async_computation.18 | async-start | bytes 25952256 | tf_op jit(solution)/shard_map/reduce_scatter | solution.py:287
  1113.6 47.2 %copy-start.88 = (f32[384]{0:T(512)S(1)}, f32[384]{0:T(512)}, u32[]{:S(2)}) copy-start(f32[384]{0:T(512)} %get-tuple-element.60) | copy-start | bytes 4612
  1113.6 47.2 %copy-start.65 = (bf16[1,384,1536]{2,1,0:T(8,128)(2,1)S(1)}, bf16[1,384,1536]{2,1,0:T(8,128)(2,1)}, u32[]{:S(2)}) copy-start(bf16[1,384,1536]{2,1,0:T(8,128)(2,1)} %get-tuple-element.92) | copy-start | bytes 3538948
  1113.6 50.3 %copy-start.18 = (f32[384,1536]{1,0:T(8,128)S(1)}, f32[384,1536]{1,0:T(8,128)}, u32[]{:S(2)}) copy-start(f32[384,1536]{1,0:T(8,128)} %copy-done.17) | copy-start | bytes 7077892
  1113.6 50.3 %copy-start.73 = (f32[1536]{0:T(1024)S(1)}, f32[1536]{0:T(1024)}, u32[]{:S(2)}) copy-start(f32[1536]{0:T(1024)} %convert_element_type.225) | copy-start | bytes 18436
  1113.6 50.3 %copy-start.81 = (f32[384]{0:T(512)S(1)}, f32[384]{0:T(512)}, u32[]{:S(2)}) copy-start(f32[384]{0:T(512)} %get-tuple-element.125) | copy-start | bytes 4612
  1167.4 827.9 %copy-start.1 = (bf16[32,12]{0,1:T(8,128)(2,1)S(1)}, bf16[32,12]{0,1:T(8,128)(2,1)}, u32[]{:S(2)}) copy-start(bf16[32,12]{0,1:T(8,128)(2,1)} %param.31) | copy-start | bytes 2308
  (69 other events, 285.0 us)
Sparse Core Ops, SparseCore 0:
  11.0 61.7 all-gather.9
  75.6 57.9 all-gather.11
  136.5 57.8 all-gather.7
  197.1 57.8 all-gather.13
  257.8 94.7 all-gather.15
  355.4 94.2 all-gather.17
  452.6 94.2 all-gather.19
  764.8 112.5 reduce-scatter.13
  884.5 113.8 reduce-scatter.11
  1004.5 113.5 reduce-scatter.9
  1125.2 113.4 reduce-scatter.7
  1245.6 244.6 reduce-scatter.19
  1498.4 245.0 reduce-scatter.17
  1750.3 245.0 reduce-scatter.15
where the time goes:
time: 2020 us; the launch traced here: 2000 us
  waiting for transfers between devices  1080 us (53%)
  local copies, waits for them, and re-layouts  382 us (19%)
  matrix products  356 us (18%)
  blocking collectives  123 us (6%)
  other arithmetic  41 us (2%)
    reduce_scatter x1, waiting for transfers between devices, body(): lax.psum_scatter(totals[7], ('fsdp', 'dp'), scatter_dimension=0, tiled=True)  253 us
    reduce_scatter x1, waiting for transfers between devices, body(): lax.psum_scatter(totals[6], ('fsdp', 'dp'), scatter_dimension=0, tiled=True)  252 us
    reduce_scatter x1, waiting for transfers between devices, body(): lax.psum_scatter(totals[8], ('fsdp', 'dp'), scatter_dimension=0, tiled=True)  252 us
    add x6, local copies, waits for them, and re-layouts, body(): jax.tree.map(jnp.add, totals, step_set)  173 us
    dot_general x14, matrix products, over_tokens(): lax.dot_general(former, latter, (((0,), (0,)), ((), ())), preferred_eleme...  122 us
    dot_general x14, matrix products, times_rows(): return jnp.dot(former, latter, preferred_element_type=jnp.float32)  104 us
    reshape x7, local copies, waits for them, and re-layouts, assemble(): jnp.transpose(shaped, (0, 2, 1, 3))  99.8 us
    dot_general x14, matrix products, times_transpose(): lax.dot_general(former, latter, (((1,), (1,)), ((), ())), preferred_eleme...  84 us
  transfers between devices with their start and end apart: 14, of which 10 were waited for; matrix products, arithmetic and copies ran while one was open for 27% of the time, Pallas kernels for 0%

commit v1 on v0

--- a/solution.py
+++ b/solution.py
@@ -6,6 +6,18 @@
 EPS = 1e-06
 NEG = -1000000000.0
 HIGH = lax.Precision.HIGHEST
+
+
+def gather_by_bits(value, axis, dim):
+    ways, here, hop = (lax.axis_size(axis), lax.axis_index(axis), value.shape[dim])
+    line, have = (value, 1)
+    while have < ways:
+        line = jnp.concatenate(
+            [line, lax.ppermute(line, axis, [(d, (d - have) % ways) for d in range(ways)])],
+            axis=dim,
+        )
+        have = 2 * have
+    return jnp.roll(line, here * hop, axis=dim)
 
 
 def times_rows(former, latter):
@@ -134,7 +146,7 @@
                 lax.all_gather(first_gain, ("fsdp", "dp"), axis=0, tiled=True),
                 lax.all_gather(query_weight, ("fsdp", "dp"), axis=0, tiled=True),
                 lax.all_gather(key_weight, ("fsdp", "dp"), axis=0, tiled=True),
-                lax.all_gather(value_weight, ("fsdp", "dp"), axis=0, tiled=True),
+                gather_by_bits(value_weight, ("fsdp", "dp"), 0),
                 lax.all_gather(output_weight, ("fsdp", "dp"), axis=0, tiled=True),
             )
         )

time: 2020 us -> 2110 us (1.045)
  blocking collectives: 123 us -> 162 us
    reduce_scatter x1, waiting for transfers between devices: 0.01 us -> 117 us  [body(): lax.psum_scatter(totals[4], ('fsdp', 'dp'), scatter_dimension=0, tiled=True)]
    reduce_scatter x1, waiting for transfers between devices: 69.7 us -> 0.01 us  [body(): lax.psum_scatter(totals[1], ('fsdp', 'dp'), scatter_dimension=0, tiled=True)]
    all_gather x1, waiting for transfers between devices: 49.1 us -> 0.02 us  [body(): lax.all_gather(output_weight, ('fsdp', 'dp'), axis=0, tiled=True)]
    psum x1, blocking collectives: 42.2 us -> 81.8 us  [body(): valid_total = lax.psum(jnp.sum(valid_float), ('fsdp', 'dp'))]
    all_gather x1, waiting for transfers between devices: 24.9 us -> 58.7 us  [body(): lax.all_gather(gate_weight, ('fsdp', 'dp'), axis=0, tiled=True)]
    ppermute x0 -> x5, waiting for transfers between devices: none -> 31.7 us  [gather_by_bits(): lax.ppermute(line, axis, [(d, (d - have) % ways) for d in range(ways)])]
    all_gather x1, waiting for transfers between devices: 49.3 us -> 22.7 us  [body(): lax.all_gather(value_weight, ('fsdp', 'dp'), axis=0, tiled=True)]
    reshape x7 -> x8, local copies, waits for them, and re-layouts: 68.8 us -> 77 us  [assemble(): shaped = gathered.reshape(fsdp_count, dp_count, row_block, col_block)]
  transfers between devices with their start and end apart: 14 -> 19, of which waited for: 10 -> 12; matrix products, arithmetic and copies ran while one was open for 27% -> 25% of each run, Pallas kernels for 0% -> 0%
where the time goes in v1:
time: 2110 us; the launch traced here: 2100 us
  waiting for transfers between devices  1100 us (52%)
  local copies, waits for them, and re-layouts  403 us (19%)
  matrix products  359 us (17%)
  blocking collectives  162 us (8%)
  other arithmetic  41.7 us (2%)
    reduce_scatter x1, waiting for transfers between devices, body(): lax.psum_scatter(totals[7], ('fsdp', 'dp'), scatter_dimension=0, tiled=True)  253 us
    reduce_scatter x1, waiting for transfers between devices, body(): lax.psum_scatter(totals[8], ('fsdp', 'dp'), scatter_dimension=0, tiled=True)  252 us
    reduce_scatter x1, waiting for transfers between devices, body(): lax.psum_scatter(totals[6], ('fsdp', 'dp'), scatter_dimension=0, tiled=True)  252 us
    add x6, local copies, waits for them, and re-layouts, body(): jax.tree.map(jnp.add, totals, step_set)  173 us
    dot_general x14, matrix products, over_tokens(): lax.dot_general(former, latter, (((0,), (0,)), ((), ())), preferred_eleme...  122 us
    reduce_scatter x1, waiting for transfers between devices, body(): lax.psum_scatter(totals[4], ('fsdp', 'dp'), scatter_dimension=0, tiled=True)  117 us
    reshape x8, local copies, waits for them, and re-layouts, assemble(): jnp.transpose(shaped, (0, 2, 1, 3))  106 us
    dot_general x14, matrix products, times_rows(): return jnp.dot(former, latter, preferred_element_type=jnp.float32)  100 us
  transfers between devices with their start and end apart: 19, of which 12 were waited for; matrix products, arithmetic and copies ran while one was open for 25% of the time, Pallas kernels for 0%

profile of v1, /device:TPU:0, one launch (start us, length us, event | category | flops | bytes accessed | tf_op | source)
XLA Modules:
  0.0 2104.0 jit_solution(17442927298840282940)
XLA Ops:
  13.0 6.4 collective-permute-start
  27.6 7.6 collective-permute-done.2
  40.6 16.9 collective-permute-done.3
  62.4 81.8 %psum.22 = f32[]{:T(128)} all-reduce(f32[]{:T(128)} %convert_reduce_fusion), channel_id=1, replica_groups=mesh['fsdp'=8,'dp'=4] {'fsdp','dp'}, use_global_device_ids=true, to_apply=%region_12.14 | all-reduce | flops 1 | bytes 8 | tf_op jit(solution)/shard_map/psum | solution.py:106
  144.7 40.8 %all-reduce.5 = (bf16[1536]{0:T(1024)(128)(2,1)S(1)}, bf16[1536]{0:T(1024)(128)(2,1)S(1)}) all-reduce(bf16[1536]{0:T(1024)(128)(2,1)S(1)} %dynamic-update-slice, bf16[1536]{0:T(1024)(128)(2,1)S(1)} %dynamic-update-slice.1), channel_id=1, replica_groups=mesh['fsdp'=8,'dp'=4] {'fsdp','dp'}, use_global_device_ids=true, to_apply=%add | all-reduce | flops 3072 | bytes 12288
  204.6 7.5 reshape.535
  285.0 22.7 %all-gather.20.cloned.1.call-done = bf16[6144,192]{1,0:T(8,128)(2,1)} async-done(((bf16[192,192]{1,0:T(8,128)(2,1)}), bf16[6144,192]{1,0:T(8,128)(2,1)}) %all-gather.20.cloned.1.call-update) | async-done | bytes 2359312 | tf_op jit(solution)/shard_map/all_gather | solution.py:225
  319.6 7.5 fusion.121
  346.6 58.7 %all-gather.14.cloned.1.call-done = bf16[6144,992]{1,0:T(8,128)(2,1)} async-done(((bf16[192,992]{1,0:T(8,128)(2,1)}), bf16[6144,992]{1,0:T(8,128)(2,1)}) %all-gather.14.cloned.1.call-update) | async-done | bytes 12189712 | tf_op jit(solution)/shard_map/all_gather | solution.py:177
  405.3 15.7 copy.223
  421.0 25.0 %reshape.548 = bf16[1536,3968]{1,0:T(8,128)(2,1)} reshape(bf16[8,192,4,992]{3,2,1,0:T(4,128)(2,1)} %bitcast.403) | data formatting | bytes 24379392 | tf_op jit(solution)/shard_map/reshape | solution.py:43
  446.0 56.4 %all-gather.16.cloned.1.call-done = bf16[6144,992]{1,0:T(8,128)(2,1)} async-done(((bf16[192,992]{1,0:T(8,128)(2,1)}), bf16[6144,992]{1,0:T(8,128)(2,1)}) %all-gather.16.cloned.1.call-update) | async-done | bytes 12189712 | tf_op jit(solution)/shard_map/all_gather | solution.py:178
  502.3 15.6 copy.222
  518.0 25.0 %reshape.550 = bf16[1536,3968]{1,0:T(8,128)(2,1)} reshape(bf16[8,192,4,992]{3,2,1,0:T(4,128)(2,1)} %bitcast.404) | data formatting | bytes 24379392 | tf_op jit(solution)/shard_map/reshape | solution.py:43
  543.0 56.5 %all-gather.18.cloned.1.call-done = bf16[6144,992]{1,0:T(8,128)(2,1)} async-done(((bf16[192,992]{1,0:T(8,128)(2,1)}), bf16[6144,992]{1,0:T(8,128)(2,1)}) %all-gather.18.cloned.1.call-update) | async-done | bytes 12189712 | tf_op jit(solution)/shard_map/all_gather | solution.py:179
  599.5 15.6 copy.221
  615.1 25.0 %reshape.552 = bf16[1536,3968]{1,0:T(8,128)(2,1)} reshape(bf16[8,192,4,992]{3,2,1,0:T(4,128)(2,1)} %bitcast.405) | data formatting | bytes 24379392 | tf_op jit(solution)/shard_map/reshape | solution.py:43
  640.1 11.8 fusion.123
  651.9 12.3 fusion.122
  664.2 9.2 multiply_convert_fusion.4
  673.5 10.8 multiply_convert_fusion.5
  684.3 9.9 convolution_add_fusion.11
  694.2 13.6 fusion.74
  707.9 17.3 multiply_convert_fusion.3
  725.1 11.1 fusion.124
  736.2 15.5 multiply_convert_fusion.2
  751.7 11.1 fusion.126
  762.9 9.9 convolution_add_fusion.10
  772.8 19.3 multiply_reduce_fusion.2
  802.0 7.7 multiply_reduce_fusion.1
  825.4 7.6 multiply_reduce_fusion
  892.1 13.7 fusion.132
  905.8 17.5 convolution_add_fusion.2
  923.3 32.5 %add.295 = f32[8,192,4,992]{3,2,1,0:T(4,128)} reshape(f32[1536,3968]{1,0:T(8,128)} %convolution_add_fusion.2) | data formatting | bytes 48758784 | tf_op jit(solution)/shard_map/add | solution.py:291
  955.9 25.0 %copy.184 = f32[8,4,192,992]{3,2,1,0:T(8,128)} copy(f32[8,4,192,992]{3,1,2,0:T(4,128)} %bitcast.400) | data formatting | bytes 48758784 | tf_op jit(solution)/shard_map/add | solution.py:291
  981.1 13.7 fusion.133
  994.8 17.8 convolution_add_fusion.1
  1012.6 32.6 %add.299 = f32[8,192,4,992]{3,2,1,0:T(4,128)} reshape(f32[1536,3968]{1,0:T(8,128)} %convolution_add_fusion.1) | data formatting | bytes 48758784 | tf_op jit(solution)/shard_map/add | solution.py:291
  1045.2 25.1 %copy.185 = f32[8,4,192,992]{3,2,1,0:T(8,128)} copy(f32[8,4,192,992]{3,1,2,0:T(4,128)} %bitcast.401) | data formatting | bytes 48758784 | tf_op jit(solution)/shard_map/add | solution.py:291
  1070.6 13.9 fusion.107
  1084.5 17.0 convolution_add_fusion
  1101.5 32.8 %add.303 = f32[8,192,4,992]{3,2,1,0:T(4,128)} reshape(f32[1536,3968]{1,0:T(8,128)} %convolution_add_fusion) | data formatting | bytes 48758784 | tf_op jit(solution)/shard_map/add | solution.py:291
  1134.2 25.3 %copy.186 = f32[8,4,192,992]{3,2,1,0:T(8,128)} copy(f32[8,4,192,992]{3,1,2,0:T(4,128)} %bitcast.402) | data formatting | bytes 48758784 | tf_op jit(solution)/shard_map/add | solution.py:291
  1170.9 39.4 %all-reduce.4 = (f32[]{:T(128)}, f32[1536]{0:T(1024)}, f32[1536]{0:T(1024)}, f32[32,12]{0,1:T(8,128)}) all-reduce(f32[]{:T(128)S(6)} %add.265, f32[1536]{0:T(1024)} %add.280, f32[1536]{0:T(1024)} %add.293, f32[32,12]{0,1:T(8,128)} %fusion.99), channel_id=1, replica_groups=mesh['fsdp'=8,'dp'=4] {'fsdp','dp'}, use_global_device_ids=true, to_apply=%region_10.12 | all-reduce | flops 3457 | bytes 27656 | tf_op jit(solution)/shard_map/psum | solution.py:303
  1222.0 117.4 %reduce-scatter.14.cloned.1.call-done = f32[192,192]{1,0:T(8,128)} async-done(((f32[6144,192]{1,0:T(8,128)}), f32[192,192]{1,0:T(8,128)}) %reduce-scatter.14.cloned.1.call-update) | async-done | bytes 147472 | tf_op jit(solution)/shard_map/reduce_scatter | solution.py:297
  1339.5 251.5 %reduce-scatter.16.cloned.1.call-done = f32[192,992]{1,0:T(8,128)} async-done(((f32[6144,992]{1,0:T(8,128)}), f32[192,992]{1,0:T(8,128)}) %reduce-scatter.16.cloned.1.call-update) | async-done | bytes 761872 | tf_op jit(solution)/shard_map/reduce_scatter | solution.py:299
  1591.0 253.2 %reduce-scatter.18.cloned.1.call-done = f32[192,992]{1,0:T(8,128)} async-done(((f32[6144,992]{1,0:T(8,128)}), f32[192,992]{1,0:T(8,128)}) %reduce-scatter.18.cloned.1.call-update) | async-done | bytes 761872 | tf_op jit(solution)/shard_map/reduce_scatter | solution.py:300
  1844.1 251.9 %reduce-scatter.20.cloned.1.call-done = f32[192,992]{1,0:T(8,128)} async-done(((f32[6144,992]{1,0:T(8,128)}), f32[192,992]{1,0:T(8,128)}) %reduce-scatter.20.cloned.1.call-update) | async-done | bytes 761872 | tf_op jit(solution)/shard_map/reduce_scatter | solution.py:301
  (359 shorter events, 252.4 us)
Async XLA Ops:
  7.2 182.5 %copy-start = (bf16[32,12]{0,1:T(8,128)(2,1)S(1)}, bf16[32,12]{0,1:T(8,128)(2,1)}, u32[]{:S(2)}) copy-start(bf16[32,12]{0,1:T(8,128)(2,1)} %param.33) | copy-start | bytes 2308
  7.2 32.8 %copy-start.75 = (s32[2,1,384]{2,1,0:T(1,128)S(1)}, s32[2,1,384]{2,1,0:T(1,128)}, u32[]{:S(2)}) copy-start(s32[2,1,384]{2,1,0:T(1,128)} %param.21) | copy-start | bytes 9220
  7.2 32.8 %copy-start.90 = (s32[2,1,384]{2,1,0:T(1,128)S(1)}, s32[2,1,384]{2,1,0:T(1,128)}, u32[]{:S(2)}) copy-start(s32[2,1,384]{2,1,0:T(1,128)} %param.22) | copy-start | bytes 9220
  7.2 222.6 %all-gather.8.cloned.1.call-start = ((), (), s32[]{:S(2)}) async-start(), calls=%async_computation.7 | async-start | bytes 3244032 | tf_op jit(solution)/shard_map/all_gather | solution.py:147
  7.9 236.9 %all-gather.10.cloned.1.call-start = ((), (), s32[]{:S(2)}) async-start(), calls=%async_computation.8 | async-start | bytes 3244032 | tf_op jit(solution)/shard_map/all_gather | solution.py:148
  8.7 253.0 %all-gather.12.cloned.1.call-start = ((), (), s32[]{:S(2)}) async-start(), calls=%async_computation.9 | async-start | bytes 3244032 | tf_op jit(solution)/shard_map/all_gather | solution.py:150
  9.4 298.3 %all-gather.20.cloned.1.call-start = ((), (), s32[]{:S(2)}) async-start(), calls=%async_computation.13 | async-start | bytes 3244032 | tf_op jit(solution)/shard_map/all_gather | solution.py:225
  10.0 395.3 %all-gather.14.cloned.1.call-start = ((), (), s32[]{:S(2)}) async-start(), calls=%async_computation.10 | async-start | bytes 12976128 | tf_op jit(solution)/shard_map/all_gather | solution.py:177
  10.6 491.7 %all-gather.16.cloned.1.call-start = ((), (), s32[]{:S(2)}) async-start(), calls=%async_computation.11 | async-start | bytes 12976128 | tf_op jit(solution)/shard_map/all_gather | solution.py:178
  11.2 588.3 %all-gather.18.cloned.1.call-start = ((), (), s32[]{:S(2)}) async-start(), calls=%async_computation.12 | async-start | bytes 12976128 | tf_op jit(solution)/shard_map/all_gather | solution.py:179
  11.9 1210.1 %reduce-scatter.8.cloned.1.call-start = ((), (), s32[]{:S(2)}) async-start(), calls=%async_computation.14 | async-start | bytes 6488064 | tf_op jit(solution)/shard_map/reduce_scatter | solution.py:294
  13.0 131.3 %copy-start.93 = (bf16[48]{0:T(256)(128)(2,1)S(1)}, bf16[48]{0:T(256)(128)(2,1)}, u32[]{:S(2)}) copy-start(bf16[48]{0:T(256)(128)(2,1)} %param.24) | copy-start | bytes 292
  13.0 131.5 %copy-start.94 = (bf16[48]{0:T(256)(128)(2,1)S(1)}, bf16[48]{0:T(256)(128)(2,1)}, u32[]{:S(2)}) copy-start(bf16[48]{0:T(256)(128)(2,1)} %param.29) | copy-start | bytes 292
  13.0 8.6 collective-permute-start
  21.7 5.6 collective-permute-start.1
  27.4 158.1 %copy-start.58 = (bf16[384,192]{0,1:T(8,128)(2,1)}, bf16[384,192]{0,1:T(8,128)(2,1)S(1)}, u32[]{:S(2)}) copy-start(bf16[384,192]{0,1:T(8,128)(2,1)S(1)} %collective-permute-done.1) | copy-start | bytes 442372
  27.5 160.0 %copy-start.4 = (bf16[2,1,384,1536]{3,2,1,0:T(8,128)(2,1)S(1)}, bf16[2,1,384,1536]{3,2,1,0:T(8,128)(2,1)}, u32[]{:S(2)}) copy-start(bf16[2,1,384,1536]{3,2,1,0:T(8,128)(2,1)} %param.18) | copy-start | bytes 7077892
  27.5 7.7 collective-permute-start.2
  36.2 21.3 %collective-permute-start.3 = (bf16[1536,192]{0,1:T(8,128)(2,1)}, bf16[1536,192]{0,1:T(8,128)(2,1)}, u32[]{:S(2)}, u32[]{:S(2)}) collective-permute-start(bf16[1536,192]{0,1:T(8,128)(2,1)} %concatenate.33), channel_id=1, source_target_pairs={{0,24},{1,25},{2,26},{3,27},{4,28},{5,29},{6,30},{7,31},{8,0},{9,1... | collective-permute-start | bytes 1769480 | tf_op jit(solution)/shard_map/ppermute | solution.py:16
  60.6 134.4 %collective-permute-start.4 = (bf16[3072,192]{0,1:T(8,128)(2,1)}, bf16[3072,192]{0,1:T(8,128)(2,1)}, u32[]{:S(2)}, u32[]{:S(2)}) collective-permute-start(bf16[3072,192]{0,1:T(8,128)(2,1)} %concatenate.34), channel_id=1, source_target_pairs={{0,16},{1,17},{2,18},{3,19},{4,20},{5,21},{6,22},{7,23},{8,24},{9,... | collective-permute-start | bytes 3538952 | tf_op jit(solution)/shard_map/ppermute | solution.py:16
  185.5 40.4 %copy-start.69 = (f32[1536]{0:T(1024)}, f32[1536]{0:T(1024)S(1)}, u32[]{:S(2)}) copy-start(f32[1536]{0:T(1024)S(1)} %convert_element_type.225) | copy-start | bytes 18436
  186.8 159.3 %copy-start.67 = (f32[1536]{0:T(1024)}, f32[1536]{0:T(1024)S(1)}, u32[]{:S(2)}) copy-start(f32[1536]{0:T(1024)S(1)} %convert_element_type.234) | copy-start | bytes 18436
  188.7 37.2 %copy-start.79 = (f32[384]{0:T(512)}, f32[384]{0:T(512)S(1)}, u32[]{:S(2)}) copy-start(f32[384]{0:T(512)S(1)} %get-tuple-element.139) | copy-start | bytes 4612
  188.7 68.0 %copy-start.76 = (f32[384]{0:T(512)}, f32[384]{0:T(512)S(1)}, u32[]{:S(2)}) copy-start(f32[384]{0:T(512)S(1)} %get-tuple-element.117) | copy-start | bytes 4612
  244.9 89.9 %copy-start.36 = (bf16[384,768]{0,1:T(8,128)(2,1)}, bf16[384,768]{0,1:T(8,128)(2,1)S(1)}, u32[]{:S(2)}) copy-start(bf16[384,768]{0,1:T(8,128)(2,1)S(1)} %copy.168) | copy-start | bytes 1769476
  261.7 73.1 %copy-start.38 = (bf16[384,768]{0,1:T(8,128)(2,1)}, bf16[384,768]{0,1:T(8,128)(2,1)S(1)}, u32[]{:S(2)}) copy-start(bf16[384,768]{0,1:T(8,128)(2,1)S(1)} %copy.169) | copy-start | bytes 1769476
  346.6 317.6 %copy-start.24 = (bf16[384,1536]{1,0:T(8,128)(2,1)}, bf16[384,1536]{1,0:T(8,128)(2,1)S(1)}, u32[]{:S(2)}) copy-start(bf16[384,1536]{1,0:T(8,128)(2,1)S(1)} %get-tuple-element.113) | copy-start | bytes 3538948
  346.6 326.9 %copy-start.28 = (bf16[384,1536]{1,0:T(8,128)(2,1)}, bf16[384,1536]{1,0:T(8,128)(2,1)S(1)}, u32[]{:S(2)}) copy-start(bf16[384,1536]{1,0:T(8,128)(2,1)S(1)} %get-tuple-element.112) | copy-start | bytes 3538948
  640.1 24.1 %slice-start.7 = ((s8[12189696]{0:T(1024)(128)(4,1)}), s8[4194304]{0:T(1024)(128)(4,1)S(1)}, s32[]{:S(2)}) async-start(s8[12189696]{0:T(1024)(128)(4,1)} %bitcast.424), calls=%async_computation.28 | async-start | bytes 8388608
  640.1 24.1 %slice-start.8 = ((s8[12189696]{0:T(1024)(128)(4,1)}), s8[4194304]{0:T(1024)(128)(4,1)S(1)}, s32[]{:S(2)}) async-start(s8[12189696]{0:T(1024)(128)(4,1)} %bitcast.424), calls=%async_computation.29 | async-start | bytes 8388608
  707.8 84.3 %copy-start.26 = (f32[384,1536]{1,0:T(8,128)}, f32[384,1536]{1,0:T(8,128)S(1)}, u32[]{:S(2)}) copy-start(f32[384,1536]{1,0:T(8,128)S(1)} %get-tuple-element.100) | copy-start | bytes 7077892
  725.1 37.7 %copy-start.53 = (bf16[384,3968]{1,0:T(8,128)(2,1)}, bf16[384,3968]{1,0:T(8,128)(2,1)S(1)}, u32[]{:S(2)}) copy-start(bf16[384,3968]{1,0:T(8,128)(2,1)S(1)} %get-tuple-element.98) | copy-start | bytes 9142276
  751.7 21.1 %copy-start.55 = (bf16[384,3968]{1,0:T(8,128)(2,1)}, bf16[384,3968]{1,0:T(8,128)(2,1)S(1)}, u32[]{:S(2)}) copy-start(bf16[384,3968]{1,0:T(8,128)(2,1)S(1)} %get-tuple-element.96) | copy-start | bytes 9142276
  772.8 19.4 copy-start.31
  772.8 19.4 copy-start.87
  772.8 19.4 copy-start.88
  865.2 356.8 %reduce-scatter.10.cloned.1.call-start = ((), (), s32[]{:S(2)}) async-start(), calls=%async_computation.15 | async-start | bytes 6488064 | tf_op jit(solution)/shard_map/reduce_scatter | solution.py:295
  873.0 349.0 %reduce-scatter.12.cloned.1.call-start = ((), (), s32[]{:S(2)}) async-start(), calls=%async_computation.16 | async-start | bytes 6488064 | tf_op jit(solution)/shard_map/reduce_scatter | solution.py:296
  880.5 459.0 %reduce-scatter.14.cloned.1.call-start = ((), (), s32[]{:S(2)}) async-start(), calls=%async_computation.17 | async-start | bytes 6488064 | tf_op jit(solution)/shard_map/reduce_scatter | solution.py:297
  890.8 700.1 %reduce-scatter.16.cloned.1.call-start = ((), (), s32[]{:S(2)}) async-start(), calls=%async_computation.18 | async-start | bytes 25952256 | tf_op jit(solution)/shard_map/reduce_scatter | solution.py:299
  980.9 863.3 %reduce-scatter.18.cloned.1.call-start = ((), (), s32[]{:S(2)}) async-start(), calls=%async_computation.19 | async-start | bytes 25952256 | tf_op jit(solution)/shard_map/reduce_scatter | solution.py:300
  1070.4 1025.7 %reduce-scatter.20.cloned.1.call-start = ((), (), s32[]{:S(2)}) async-start(), calls=%async_computation.20 | async-start | bytes 25952256 | tf_op jit(solution)/shard_map/reduce_scatter | solution.py:301
  1167.6 46.5 %copy-start.89 = (f32[384]{0:T(512)S(1)}, f32[384]{0:T(512)}, u32[]{:S(2)}) copy-start(f32[384]{0:T(512)} %get-tuple-element.74) | copy-start | bytes 4612
  1167.6 46.5 %copy-start.62 = (bf16[1,384,1536]{2,1,0:T(8,128)(2,1)S(1)}, bf16[1,384,1536]{2,1,0:T(8,128)(2,1)}, u32[]{:S(2)}) copy-start(bf16[1,384,1536]{2,1,0:T(8,128)(2,1)} %get-tuple-element.106) | copy-start | bytes 3538948
  1167.6 49.6 %copy-start.18 = (f32[384,1536]{1,0:T(8,128)S(1)}, f32[384,1536]{1,0:T(8,128)}, u32[]{:S(2)}) copy-start(f32[384,1536]{1,0:T(8,128)} %copy-done.17) | copy-start | bytes 7077892
  1167.7 49.6 %copy-start.73 = (f32[1536]{0:T(1024)S(1)}, f32[1536]{0:T(1024)}, u32[]{:S(2)}) copy-start(f32[1536]{0:T(1024)} %copy-done.69) | copy-start | bytes 18436
  1167.7 49.6 %copy-start.82 = (f32[384]{0:T(512)S(1)}, f32[384]{0:T(512)}, u32[]{:S(2)}) copy-start(f32[384]{0:T(512)} %copy-done.79) | copy-start | bytes 4612
  1220.4 875.6 %copy-start.1 = (bf16[32,12]{0,1:T(8,128)(2,1)S(1)}, bf16[32,12]{0,1:T(8,128)(2,1)}, u32[]{:S(2)}) copy-start(bf16[32,12]{0,1:T(8,128)(2,1)} %param.33) | copy-start | bytes 2308
  (77 other events, 390.9 us)
Sparse Core Ops, SparseCore 0:
  10.9 94.3 all-gather.7
  108.2 78.1 all-gather.9
  189.2 57.7 all-gather.11
  249.8 57.8 all-gather.19
  310.5 94.8 all-gather.13
  408.1 94.2 all-gather.15
  505.2 94.2 all-gather.17
  865.3 112.6 reduce-scatter.7
  985.1 113.5 reduce-scatter.9
  1104.8 114.2 reduce-scatter.11
  1226.2 113.2 reduce-scatter.13
  1346.3 244.6 reduce-scatter.15
  1599.1 245.0 reduce-scatter.17
  1851.0 244.9 reduce-scatter.19
